TPU v7x, 256 devices: a whole 4x4x8 slice. The times are simulated.
256 devices in a mesh: dp: 16 (over z_hi, y), fsdp: 16 (over x, z_lo, core).
Axes of the slice: x: 4, y: 4, z: 8 (z_hi: 4, z_lo: 2; z = z_hi * 2 + z_lo), core: 2. Of those that a mesh axis runs over, the one named last changes fastest.
Arguments:
- tokens: bfloat16 [32768, 4096], P(('dp', 'fsdp')), may hold values from -6 to 6
- route_ids: int32 [32768, 4], P(('dp', 'fsdp')), may hold values from 0 to 15, all different within a row; in each aligned block of 128 rows (0 to 127, 128 to 255, ...) at most 48 rows name the same one
- gate_values: float32 [32768, 4], P(('dp', 'fsdp')), may hold values from 0.1 to 1
- w_gate_up: bfloat16 [16, 4096, 1536], P('dp', 'fsdp'), may hold values from -0.09375 to 0.09375
- w_down: bfloat16 [16, 768, 4096], P('dp', None, 'fsdp'), may hold values from -0.21875 to 0.21875
Outputs:
- combined: bfloat16 [32768, 4096], P(('dp', 'fsdp'))
Inputs may be any that keep to these rules, and one draw needn't show every extreme that they name: `route_ids`: each row names 4 different experts. Among the rows of one device no expert is named by more than 48 rows, a bound that some block reaches of some device in every draw.
All inputs are finite; a program needn't handle non-finite values.
Results may differ from a plain program's by a relative error of at most 0.0058.
Values may be sent and summed in bfloat16 or wider, within the bound.
No kernel may reach another device: no remote copies, remote signals or barrier semaphores. Data moves between devices by JAX's collectives and lax.ppermute only.
A program may use at most 128 MiB of HBM per device.

v0:
```python
import jax
import jax.numpy as jnp
from jax import lax
from jax.sharding import PartitionSpec as P


def on_device(tokens, route_ids, gate_values, w_gate_up, w_down):
    dp_count = lax.axis_size("dp")
    tok_rows, top_count = route_ids.shape
    model_width = tokens.shape[1]
    hidden_units = w_down.shape[1]
    capacity = 3 * tok_rows * top_count // (2 * dp_count)
    flat_routes = route_ids.reshape(-1)
    matched = (flat_routes[:, None] == jnp.arange(dp_count, dtype=jnp.int32)[None, :]).astype(
        jnp.int32
    )
    ranked = jnp.cumsum(matched, axis=0) - 1
    slot_index = jnp.sum(ranked * matched, axis=1)
    target = flat_routes * capacity + slot_index
    owner_token = jnp.arange(tok_rows * top_count, dtype=jnp.int32) // top_count
    source = jnp.full((dp_count * capacity,), tok_rows, jnp.int32).at[target].set(owner_token)
    padded = jnp.concatenate([tokens, jnp.zeros((1, model_width), tokens.dtype)], axis=0)
    outgoing = jnp.take(padded, source, axis=0).reshape(dp_count, capacity, model_width)
    arrived = lax.all_to_all(outgoing, "dp", split_axis=0, concat_axis=0, tiled=True)
    expert_rows = arrived.reshape(dp_count * capacity, model_width)
    projected = jnp.dot(
        expert_rows,
        lax.all_gather(w_gate_up, "fsdp", axis=1, tiled=True)[0],
        preferred_element_type=jnp.float32,
    )
    hidden = (jax.nn.silu(projected[:, :hidden_units]) * projected[:, hidden_units:]).astype(
        jnp.bfloat16
    )
    produced = jnp.dot(
        hidden,
        lax.all_gather(w_down, "fsdp", axis=2, tiled=True)[0],
        preferred_element_type=jnp.float32,
    ).astype(jnp.bfloat16)
    returned = lax.all_to_all(
        produced.reshape(dp_count, capacity, model_width),
        "dp",
        split_axis=0,
        concat_axis=0,
        tiled=True,
    )
    picked = jnp.take(returned.reshape(dp_count * capacity, model_width), target, axis=0)
    picked = picked.reshape(tok_rows, top_count, model_width)
    combined = jnp.sum(gate_values[:, :, None] * picked.astype(jnp.float32), axis=1)
    return combined.astype(jnp.bfloat16)


def solution(mesh):
    in_specs = (
        P(("dp", "fsdp"), None),
        P(("dp", "fsdp"), None),
        P(("dp", "fsdp"), None),
        P("dp", "fsdp", None),
        P("dp", None, "fsdp"),
    )
    out_specs = P(("dp", "fsdp"), None)
    return jax.shard_map(
        on_device, mesh=mesh, in_specs=in_specs, out_specs=out_specs, check_vma=False
    )
```

profile of v0, /device:TPU:181, one launch (start us, length us, event | category | flops | bytes accessed | tf_op | source)
XLA Modules:
  0.0 468.4 jit_solution(13075663889717124449)
XLA Ops:
  6.5 0.0 all-gather.3.cloned.1.call-start
  6.5 0.7 all-gather.3.cloned.1.call-update
  7.3 0.8 copy.14
  8.0 0.1 eq.26
  8.2 0.1 reshape.86
  8.3 1.2 reduce-window.6
  9.4 0.2 slice_reduce_fusion
  9.7 0.7 broadcast_multiply_fusion
  10.4 0.1 copy.19
  10.5 0.1 mul.41
  10.6 0.1 fusion.7
  10.7 2.4 scatter_custom_fusion
  13.2 0.1 broadcast_in_dim.33
  13.3 1.3 concatenate.3
  14.6 5.8 %gather_fusion = bf16[768,4096]{1,0:T(8,128)(2,1)} fusion(bf16[129,4096]{1,0:T(8,128)(2,1)S(1)} %concatenate.3, s32[1024]{0:T(1024)S(1)} %pad_clamp_fusion.1), kind=kCustom, calls=%fused_computation | custom fusion | bytes 12585984 | tf_op jit(solution)/shard_map/jit(_take)/gather | solution.py:23
  20.4 6.6 %broadcast_select_fusion = bf16[16,48,4096]{2,1,0:T(8,128)(2,1)} fusion(bf16[16,48,4096]{2,1,0:T(8,128)(2,1)} %bitcast.28, pred[16,48]{1,0:T(8,128)(4,1)S(1)} %broadcast_in_dim.33), kind=kLoop, calls=%fused_computation.8 | loop fusion | flops 3145728 | bytes 12583680 | tf_op jit(solution)/shard_map/jit(_take)/select_n | solution.py:23
  27.0 9.1 %all-to-all-start = ((bf16[16,48,4096]{2,1,0:T(8,128)(2,1)}), bf16[16,48,4096]{2,1,0:T(8,128)(2,1)}, u32[]{:S(2)}, u32[]{:S(2)}) async-start(bf16[16,48,4096]{2,1,0:T(8,128)(2,1)} %broadcast_select_fusion), calls=%async_computation | async-start | bytes 12582912 | tf_op jit(solution)/shard_map/all_to_all | solution.py:24
  36.1 0.0 all-gather.5.cloned.1.call-start
  36.1 0.7 all-gather.5.cloned.1.call-update
  36.8 142.0 %all-to-all-done = bf16[16,48,4096]{2,1,0:T(8,128)(2,1)} async-done(((bf16[16,48,4096]{2,1,0:T(8,128)(2,1)}), bf16[16,48,4096]{2,1,0:T(8,128)(2,1)}, u32[]{:S(2)}, u32[]{:S(2)}) %all-to-all-start) | async-done | bytes 6291488 | tf_op jit(solution)/shard_map/all_to_all | solution.py:24
  178.8 16.1 %fusion = f32[768,1536]{1,0:T(8,128)} fusion(bf16[768,4096]{1,0:T(8,128)(2,1)} %bitcast.4, bf16[1,4096,1536]{2,1,0:T(8,128)(2,1)} %all-gather.3.cloned.1.call-done), kind=kOutput, calls=%fused_computation.3 | convolution fusion | flops 9663676416 | bytes 23592960 | tf_op jit(solution)/shard_map/dot_general | solution.py:26
  195.0 62.0 %all-gather.5.cloned.1.call-done = bf16[1,768,4096]{2,1,0:T(8,128)(2,1)} async-done(((bf16[1,768,256]{2,1,0:T(8,128)(2,1)}), bf16[1,768,4096]{2,1,0:T(8,128)(2,1)}) %all-gather.5.cloned.1.call-update) | async-done | bytes 6291472 | tf_op jit(solution)/shard_map/all_gather | solution.py:36
  257.0 10.3 %convolution_convert_fusion = bf16[768,4096]{1,0:T(8,128)(2,1)} fusion(bf16[1,768,4096]{2,1,0:T(8,128)(2,1)} %all-gather.5.cloned.1.call-done, f32[768,1536]{1,0:T(8,128)} %fusion), kind=kOutput, calls=%fused_computation.6 | convolution fusion | flops 4838522880 | bytes 17301504 | tf_op jit(solution)/shard_map/dot_general | solution.py:34
  267.2 9.2 %all-to-all-start.1 = ((bf16[16,48,4096]{2,1,0:T(8,128)(2,1)}), bf16[16,48,4096]{2,1,0:T(8,128)(2,1)}, u32[]{:S(2)}, u32[]{:S(2)}) async-start(bf16[16,48,4096]{2,1,0:T(8,128)(2,1)} %bitcast.29), calls=%async_computation.1 | async-start | bytes 12582912 | tf_op jit(solution)/shard_map/all_to_all | solution.py:39
  276.4 0.1 reduce_sum.23
  276.6 0.1 copy.17
  276.7 0.1 copy.18
  276.8 0.1 copy.13
  276.9 153.0 %all-to-all-done.1 = bf16[16,48,4096]{2,1,0:T(8,128)(2,1)} async-done(((bf16[16,48,4096]{2,1,0:T(8,128)(2,1)}), bf16[16,48,4096]{2,1,0:T(8,128)(2,1)}, u32[]{:S(2)}, u32[]{:S(2)}) %all-to-all-start.1) | async-done | bytes 6291488 | tf_op jit(solution)/shard_map/all_to_all | solution.py:39
  429.9 12.2 %gather_fusion.1 = bf16[512,4096]{1,0:T(8,128)(2,1)} fusion(bf16[768,4096]{1,0:T(8,128)(2,1)} %bitcast.8, s32[1024]{0:T(1024)S(1)} %pad_clamp_fusion), kind=kCustom, calls=%fused_computation.1 | custom fusion | bytes 8390656 | tf_op jit(solution)/shard_map/jit(_take)/gather | solution.py:46
  442.0 7.2 %gather.15 = bf16[128,4,4096]{2,1,0:T(4,128)(2,1)} reshape(bf16[512,4096]{1,0:T(8,128)(2,1)} %gather_fusion.1) | data formatting | bytes 8388608 | tf_op jit(solution)/shard_map/jit(_take)/gather | solution.py:46
  449.2 12.3 %multiply_reduce_fusion = bf16[128,4096]{1,0:T(8,128)(2,1)} fusion(bf16[128,4,4096]{2,1,0:T(4,128)(2,1)} %gather.15, f32[128,4]{1,0:T(8,128)S(1)} %copy.13, pred[128,4]{1,0:T(8,128)(4,1)S(1)} %copy.18), kind=kLoop, calls=%fused_computation.5 | loop fusion | flops 7864320 | bytes 5245440 | tf_op jit(solution)/shard_map/reduce_sum | solution.py:48
  (15 shorter events, 0.1 us)
Async XLA Ops:
  6.5 172.3 %all-gather.3.cloned.1.call-start = ((), (), s32[]{:S(2)}) async-start(), calls=%async_computation.2 | async-start | bytes 13369344 | tf_op jit(solution)/shard_map/all_gather | solution.py:28
  27.0 151.8 %all-to-all-start = ((bf16[16,48,4096]{2,1,0:T(8,128)(2,1)}), bf16[16,48,4096]{2,1,0:T(8,128)(2,1)}, u32[]{:S(2)}, u32[]{:S(2)}) async-start(bf16[16,48,4096]{2,1,0:T(8,128)(2,1)} %broadcast_select_fusion), calls=%async_computation | async-start | bytes 12582912 | tf_op jit(solution)/shard_map/all_to_all | solution.py:24
  36.1 220.9 %all-gather.5.cloned.1.call-start = ((), (), s32[]{:S(2)}) async-start(), calls=%async_computation.3 | async-start | bytes 6684672 | tf_op jit(solution)/shard_map/all_gather | solution.py:36
  267.2 9.4 %copy-start = (s32[128,4]{0,1:T(4,128)S(1)}, s32[128,4]{0,1:T(4,128)}, u32[]{:S(2)}) copy-start(s32[128,4]{0,1:T(4,128)} %param.6) | copy-start | bytes 6148
  267.2 9.6 %copy-start.1 = (f32[128,4]{0,1:T(4,128)S(1)}, f32[128,4]{0,1:T(4,128)}, u32[]{:S(2)}) copy-start(f32[128,4]{0,1:T(4,128)} %param.7) | copy-start | bytes 6148
  267.2 162.6 %all-to-all-start.1 = ((bf16[16,48,4096]{2,1,0:T(8,128)(2,1)}), bf16[16,48,4096]{2,1,0:T(8,128)(2,1)}, u32[]{:S(2)}, u32[]{:S(2)}) async-start(bf16[16,48,4096]{2,1,0:T(8,128)(2,1)} %bitcast.29), calls=%async_computation.1 | async-start | bytes 12582912 | tf_op jit(solution)/shard_map/all_to_all | solution.py:39
Sparse Core Ops, SparseCore 0:
  9.2 158.8 all-gather.2
  169.8 87.0 all-gather.4
where the time goes:
time: 469 us; the launch traced here: 468 us
  waiting for transfers between devices  358 us (76%)
  local copies, waits for them, and re-layouts  30.8 us (7%)
  matrix products  26.4 us (6%)
  other arithmetic  21 us (4%)
  starting transfers between devices  18.3 us (4%)
  between operations  13.5 us (3%)
    all_to_all x1, waiting for transfers between devices, on_device(): lax.all_to_all(produced.reshape(dp_count, capacity, model_width), 'dp', s...  153 us
    all_to_all x1, waiting for transfers between devices, on_device(): lax.all_to_all(outgoing, 'dp', split_axis=0, concat_axis=0, tiled=True)  142 us
    all_gather x1, waiting for transfers between devices, on_device(): lax.all_gather(w_down, 'fsdp', axis=2, tiled=True)[0]  62 us
    gather x2, local copies, waits for them, and re-layouts, on_device(): jnp.take(returned.reshape(dp_count * capacity, model_width), target, axis=0)  19.3 us
    dot_general x1, matrix products, on_device(): jnp.dot(expert_rows, lax.all_gather(w_gate_up, 'fsdp', axis=1, tiled=True...  16.1 us
    reduce_sum x1, other arithmetic, on_device(): jnp.sum(gate_values[:, :, None] * picked.astype(jnp.float32), axis=1)  12.3 us
    dot_general x1, matrix products, on_device(): jnp.dot(hidden, lax.all_gather(w_down, 'fsdp', axis=2, tiled=True)[0], pr...  10.3 us
  transfers between devices with their start and end apart: 4, of which 3 were waited for; matrix products, arithmetic and copies ran while one was open for 8% of the time, Pallas kernels for 0%

commit v1 on v0

--- a/solution.py
+++ b/solution.py
@@ -33,7 +33,9 @@
     )
     produced = jnp.dot(
         hidden,
-        lax.all_gather(w_down, "fsdp", axis=2, tiled=True)[0],
+        jnp.concatenate(
+            lax.all_to_all(jnp.stack([w_down] * lax.axis_size("fsdp")), "fsdp", 0, 0), axis=2
+        )[0],
         preferred_element_type=jnp.float32,
     ).astype(jnp.bfloat16)
     returned = lax.all_to_all(

time: 469 us -> 508 us (1.083); the launches traced: 468 us -> 501 us
  starting transfers between devices: 18.3 us -> 63.8 us
  waiting for transfers between devices: 358 us -> 342 us
    all_gather x1 -> x0, waiting for transfers between devices: 62 us -> none  [on_device(): lax.all_gather(w_down, 'fsdp', axis=2, tiled=True)[0]]
    all_to_all x0 -> x1, waiting for transfers between devices: none -> 53.8 us  [on_device(): lax.all_to_all(jnp.stack([w_down] * lax.axis_size('fsdp')), 'fsdp', 0, 0)]
    all_to_all x0 -> x1, starting transfers between devices: none -> 44.5 us  [on_device(): lax.all_to_all(jnp.stack([w_down] * lax.axis_size('fsdp')), 'fsdp', 0, 0)]
    all_to_all x1, waiting for transfers between devices: 153 us -> 145 us  [on_device(): lax.all_to_all(produced.reshape(dp_count, capacity, model_width), 'dp', s...]
where the time goes in v1:
time: 508 us; the launch traced here: 501 us
  waiting for transfers between devices  342 us (67%)
  starting transfers between devices  63.8 us (13%)
  local copies, waits for them, and re-layouts  34.3 us (7%)
  matrix products  26.4 us (5%)
  other arithmetic  20.9 us (4%)
  between operations  13.5 us (3%)
    all_to_all x1, waiting for transfers between devices, on_device(): lax.all_to_all(produced.reshape(dp_count, capacity, model_width), 'dp', s...  145 us
    all_to_all x1, waiting for transfers between devices, on_device(): lax.all_to_all(outgoing, 'dp', split_axis=0, concat_axis=0, tiled=True)  143 us
    all_to_all x1, waiting for transfers between devices, on_device(): lax.all_to_all(jnp.stack([w_down] * lax.axis_size('fsdp')), 'fsdp', 0, 0)  53.8 us
    all_to_all x1, starting transfers between devices, on_device(): lax.all_to_all(jnp.stack([w_down] * lax.axis_size('fsdp')), 'fsdp', 0, 0)  44.5 us
    gather x2, local copies, waits for them, and re-layouts, on_device(): jnp.take(returned.reshape(dp_count * capacity, model_width), target, axis=0)  19.3 us
    dot_general x1, matrix products, on_device(): jnp.dot(expert_rows, lax.all_gather(w_gate_up, 'fsdp', axis=1, tiled=True...  16.1 us
    reduce_sum x1, other arithmetic, on_device(): jnp.sum(gate_values[:, :, None] * picked.astype(jnp.float32), axis=1)  12.3 us
    dot_general x1, matrix products, on_device(): jnp.dot(hidden, jnp.concatenate(lax.all_to_all(jnp.stack([w_down] * lax.a...  10.3 us
  transfers between devices with their start and end apart: 4, of which 3 were waited for; matrix products, arithmetic and copies ran while one was open for 8% of the time, Pallas kernels for 0%

profile of v1, /device:TPU:181, one launch (start us, length us, event | category | flops | bytes accessed | tf_op | source)
XLA Modules:
  0.0 500.7 jit_solution(2690201148545989446)
XLA Ops:
  6.5 0.7 all-gather.2.cloned.1.call-update
  7.3 0.8 copy.22
  8.0 0.1 eq.26
  8.2 0.1 reshape.92
  8.3 1.2 reduce-window.6
  9.4 0.2 slice_reduce_fusion
  9.7 0.7 broadcast_multiply_fusion
  10.4 0.1 copy.27
  10.5 0.1 mul.41
  10.6 0.1 fusion.6
  10.7 2.4 scatter_custom_fusion
  13.2 0.1 broadcast_in_dim.33
  13.3 1.3 concatenate.3
  14.6 5.8 %gather_fusion = bf16[768,4096]{1,0:T(8,128)(2,1)} fusion(bf16[129,4096]{1,0:T(8,128)(2,1)S(1)} %concatenate.3, s32[1024]{0:T(1024)S(1)} %pad_clamp_fusion.1), kind=kCustom, calls=%fused_computation | custom fusion | bytes 12585984 | tf_op jit(solution)/shard_map/jit(_take)/gather | solution.py:23
  20.4 6.5 %broadcast_select_fusion = bf16[16,48,4096]{2,1,0:T(8,128)(2,1)} fusion(bf16[16,48,4096]{2,1,0:T(8,128)(2,1)} %bitcast.32, pred[16,48]{1,0:T(8,128)(4,1)S(1)} %broadcast_in_dim.33), kind=kLoop, calls=%fused_computation.7 | loop fusion | flops 3145728 | bytes 12583680 | tf_op jit(solution)/shard_map/jit(_take)/select_n | solution.py:23
  26.9 9.2 %all-to-all-start = ((bf16[16,48,4096]{2,1,0:T(8,128)(2,1)}), bf16[16,48,4096]{2,1,0:T(8,128)(2,1)}, u32[]{:S(2)}, u32[]{:S(2)}) async-start(bf16[16,48,4096]{2,1,0:T(8,128)(2,1)} %broadcast_select_fusion), calls=%async_computation | async-start | bytes 12582912 | tf_op jit(solution)/shard_map/all_to_all | solution.py:24
  36.1 0.2 copy.28
  36.3 142.5 %all-to-all-done = bf16[16,48,4096]{2,1,0:T(8,128)(2,1)} async-done(((bf16[16,48,4096]{2,1,0:T(8,128)(2,1)}), bf16[16,48,4096]{2,1,0:T(8,128)(2,1)}, u32[]{:S(2)}, u32[]{:S(2)}) %all-to-all-start) | async-done | bytes 6291488 | tf_op jit(solution)/shard_map/all_to_all | solution.py:24
  178.8 3.3 stack.2
  182.1 44.5 %all-to-all-start.1 = ((bf16[16,1,768,256]{2,3,1,0:T(8,128)(2,1)}), bf16[16,1,768,256]{2,3,1,0:T(8,128)(2,1)}, u32[]{:S(2)}, u32[]{:S(2)}) async-start(bf16[16,1,768,256]{2,3,1,0:T(8,128)(2,1)} %stack.2), calls=%async_computation.1 | async-start | bytes 12582912 | tf_op jit(solution)/shard_map/all_to_all | solution.py:37
  226.7 16.1 %fusion = f32[768,1536]{1,0:T(8,128)} fusion(bf16[768,4096]{1,0:T(8,128)(2,1)} %bitcast.4, bf16[1,4096,1536]{2,1,0:T(8,128)(2,1)} %all-gather.2.cloned.1.call-done), kind=kOutput, calls=%fused_computation.3 | convolution fusion | flops 9663676416 | bytes 23592960 | tf_op jit(solution)/shard_map/dot_general | solution.py:26
  242.8 53.8 %all-to-all-done.1 = bf16[16,1,768,256]{2,3,1,0:T(8,128)(2,1)} async-done(((bf16[16,1,768,256]{2,3,1,0:T(8,128)(2,1)}), bf16[16,1,768,256]{2,3,1,0:T(8,128)(2,1)}, u32[]{:S(2)}, u32[]{:S(2)}) %all-to-all-start.1) | async-done | bytes 6291488 | tf_op jit(solution)/shard_map/all_to_all | solution.py:37
  296.6 10.3 %convolution_convert_fusion = bf16[768,4096]{1,0:T(8,128)(2,1)} fusion(bf16[768,4096]{0,1:T(8,128)(2,1)} %bitcast.9, f32[768,1536]{1,0:T(8,128)} %fusion), kind=kOutput, calls=%fused_computation.6 | convolution fusion | flops 4838522880 | bytes 17301504 | tf_op jit(solution)/shard_map/dot_general | solution.py:34
  306.9 10.0 %all-to-all-start.2 = ((bf16[16,48,4096]{2,1,0:T(8,128)(2,1)}), bf16[16,48,4096]{2,1,0:T(8,128)(2,1)}, u32[]{:S(2)}, u32[]{:S(2)}) async-start(bf16[16,48,4096]{2,1,0:T(8,128)(2,1)} %bitcast.33), calls=%async_computation.2 | async-start | bytes 12582912 | tf_op jit(solution)/shard_map/all_to_all | solution.py:41
  316.9 0.1 reduce_sum.23
  317.1 0.1 copy.25
  317.2 0.1 copy.26
  317.3 0.1 copy.21
  317.4 144.8 %all-to-all-done.2 = bf16[16,48,4096]{2,1,0:T(8,128)(2,1)} async-done(((bf16[16,48,4096]{2,1,0:T(8,128)(2,1)}), bf16[16,48,4096]{2,1,0:T(8,128)(2,1)}, u32[]{:S(2)}, u32[]{:S(2)}) %all-to-all-start.2) | async-done | bytes 6291488 | tf_op jit(solution)/shard_map/all_to_all | solution.py:41
  462.2 12.2 %gather_fusion.1 = bf16[512,4096]{1,0:T(8,128)(2,1)} fusion(bf16[768,4096]{1,0:T(8,128)(2,1)} %bitcast.11, s32[1024]{0:T(1024)S(1)} %pad_clamp_fusion), kind=kCustom, calls=%fused_computation.1 | custom fusion | bytes 8390656 | tf_op jit(solution)/shard_map/jit(_take)/gather | solution.py:48
  474.4 7.2 %gather.15 = bf16[128,4,4096]{2,1,0:T(4,128)(2,1)} reshape(bf16[512,4096]{1,0:T(8,128)(2,1)} %gather_fusion.1) | data formatting | bytes 8388608 | tf_op jit(solution)/shard_map/jit(_take)/gather | solution.py:48
  481.6 12.3 %multiply_reduce_fusion = bf16[128,4096]{1,0:T(8,128)(2,1)} fusion(bf16[128,4,4096]{2,1,0:T(4,128)(2,1)} %gather.15, f32[128,4]{1,0:T(8,128)S(1)} %copy.21, pred[128,4]{1,0:T(8,128)(4,1)S(1)} %copy.26), kind=kLoop, calls=%fused_computation.5 | loop fusion | flops 7864320 | bytes 5245440 | tf_op jit(solution)/shard_map/reduce_sum | solution.py:50
  (18 shorter events, 0.1 us)
Async XLA Ops:
  6.5 220.1 %all-gather.2.cloned.1.call-start = ((), (), s32[]{:S(2)}) async-start(), calls=%async_computation.3 | async-start | bytes 13369344 | tf_op jit(solution)/shard_map/all_gather | solution.py:28
  26.9 9.2 %copy-start = (bf16[1,768,256]{2,1,0:T(8,128)(2,1)S(1)}, bf16[1,768,256]{2,1,0:T(8,128)(2,1)}, u32[]{:S(2)}) copy-start(bf16[1,768,256]{2,1,0:T(8,128)(2,1)} %param.9) | copy-start | bytes 1179652
  26.9 151.9 %all-to-all-start = ((bf16[16,48,4096]{2,1,0:T(8,128)(2,1)}), bf16[16,48,4096]{2,1,0:T(8,128)(2,1)}, u32[]{:S(2)}, u32[]{:S(2)}) async-start(bf16[16,48,4096]{2,1,0:T(8,128)(2,1)} %broadcast_select_fusion), calls=%async_computation | async-start | bytes 12582912 | tf_op jit(solution)/shard_map/all_to_all | solution.py:24
  182.1 114.5 %all-to-all-start.1 = ((bf16[16,1,768,256]{2,3,1,0:T(8,128)(2,1)}), bf16[16,1,768,256]{2,3,1,0:T(8,128)(2,1)}, u32[]{:S(2)}, u32[]{:S(2)}) async-start(bf16[16,1,768,256]{2,3,1,0:T(8,128)(2,1)} %stack.2), calls=%async_computation.1 | async-start | bytes 12582912 | tf_op jit(solution)/shard_map/all_to_all | solution.py:37
  306.9 10.2 %copy-start.1 = (s32[128,4]{0,1:T(4,128)S(1)}, s32[128,4]{0,1:T(4,128)}, u32[]{:S(2)}) copy-start(s32[128,4]{0,1:T(4,128)} %param.6) | copy-start | bytes 6148
  306.9 10.4 %copy-start.2 = (f32[128,4]{0,1:T(4,128)S(1)}, f32[128,4]{0,1:T(4,128)}, u32[]{:S(2)}) copy-start(f32[128,4]{0,1:T(4,128)} %param.7) | copy-start | bytes 6148
  306.9 155.3 %all-to-all-start.2 = ((bf16[16,48,4096]{2,1,0:T(8,128)(2,1)}), bf16[16,48,4096]{2,1,0:T(8,128)(2,1)}, u32[]{:S(2)}, u32[]{:S(2)}) async-start(bf16[16,48,4096]{2,1,0:T(8,128)(2,1)} %bitcast.33), calls=%async_computation.2 | async-start | bytes 12582912 | tf_op jit(solution)/shard_map/all_to_all | solution.py:41
Sparse Core Ops, SparseCore 0:
  9.2 158.8 all-gather.1
